TPU v7x, 32 devices: a whole 2x2x4 slice. The times are simulated.
32 devices in a mesh: zone: 4 (over y, x), dev: 8 (over z, core).
Axes of the slice: x: 2, y: 2, z: 4, core: 2. Of those that a mesh axis runs over, the one named last changes fastest.
Arguments:
- quad_weight: float32 [16384, 128], P(('zone', 'dev')), may hold values from 0.002 to 0.014
- param_coords: float32 [16384, 4, 128], P(('zone', 'dev')), may hold values from -1 to 1
- slave_points: float32 [16384, 3, 128], P(('zone', 'dev')), may hold values from -6 to 6
- slave_normals: float32 [16384, 3, 128], P(('zone', 'dev')), may hold values from -1 to 1, as said below
- block_owner: int32 [16384, 1], P(('zone', 'dev')), may hold values from 0 to 7; in each aligned block of 128 rows (0 to 127, 128 to 255, ...) at most 16 rows name the same one
- block_patch: int32 [16384], P(('zone', 'dev')), may hold values from 0 to 8191
- block_count: int32 [32, 4], P(('zone', 'dev')), may hold values from 1 to 128, as said below
- active_flags: int32 [4, 16384], P(None, ('zone', 'dev')), may hold values 0 or 1
- normal_mult: float32 [4, 16384], P(None, ('zone', 'dev')), may hold values from 0.5 to 4
- tangent_mult: float32 [12, 16384], P(None, ('zone', 'dev')), may hold values from -6 to 6
- master_patch: float32 [12, 262144], P(None, ('zone', 'dev')), may hold values from -6 to 6
Outputs:
- mortar_d: float32 [16, 16384], P(None, ('zone', 'dev'))
- mortar_m: float32 [16, 16384], P(None, ('zone', 'dev'))
- gap_lin: float32 [48, 16384], P(None, ('zone', 'dev'))
- gap_res: float32 [4, 16384], P(None, ('zone', 'dev'))
- cone_res: float32 [12, 16384], P(None, ('zone', 'dev'))
Inputs may be any that keep to these rules, and one draw needn't show every extreme that they name: Device q's live blocks toward group k are the first block_count[q, k] of its 128 slots for k; in every draw each device fills all 128 slots toward one group, the same group for all devices of one dev index. `slave_normals`: every normal has unit length. `block_owner`: in each aligned block of 128 slots (one device toward one group) no owner is named by more than 16 slots.
All inputs are finite; a program needn't handle non-finite values. No bound on the sum of `active_flags` on one device may be relied on, other than what follows from the above.
Results may differ from a plain program's by a relative error of at most 0.0003.
Values sent between devices are 32-bit elements; how exact they have to be, the bound alone decides.
A program may use at most 320 MiB of HBM per device.

v0:
```python
import jax
import jax.numpy as jnp
from jax import lax
from jax.sharding import PartitionSpec as P

BUCKET = 16
friction_coef = 0.3
newton_scale = 4.0


def bilinear(first, second):
    return jnp.stack(
        [
            0.25 * (1.0 - first) * (1.0 - second),
            0.25 * (1.0 + first) * (1.0 - second),
            0.25 * (1.0 + first) * (1.0 + second),
            0.25 * (1.0 - first) * (1.0 + second),
        ],
        axis=0,
    )


def slave_terms(weight, coords):
    shape_s = bilinear(coords[:, 2], coords[:, 3])
    weighted = weight[None] * shape_s
    return jnp.sum(weighted[:, None] * shape_s[None], axis=-1).reshape(16, -1)


def master_terms(weight, coords, points, normals, corners):
    shape_s = bilinear(coords[:, 2], coords[:, 3])
    shape_m = bilinear(coords[:, 0], coords[:, 1])
    weighted = weight[None] * shape_s
    paired = weighted[:, None] * shape_m[None]
    mortar_m = jnp.sum(paired, axis=-1).reshape(16, -1)
    diffs = []
    for direction in range(3):
        position = jnp.sum(shape_m * corners[4 * direction : 4 * direction + 4][:, :, None], axis=0)
        diffs.append(position - points[:, direction])
    gap_point = normals[:, 0] * diffs[0] + normals[:, 1] * diffs[1] + normals[:, 2] * diffs[2]
    wgap = jnp.sum(weighted * gap_point[None], axis=-1)
    slips = [
        jnp.sum(weighted * (diffs[direction] - normals[:, direction] * gap_point)[None], axis=-1)
        for direction in range(3)
    ]
    lins = [
        jnp.sum(paired * normals[:, direction][None, None], axis=-1).reshape(16, -1)
        for direction in range(3)
    ]
    return (mortar_m, wgap, jnp.concatenate(slips, axis=0), jnp.concatenate(lins, axis=0))


def residuals(wgap, wslip, active, normal_mult, tangent_mult):
    radius = friction_coef * normal_mult
    trial = tangent_mult + newton_scale * wslip
    length = jnp.sqrt(trial[0:4] * trial[0:4] + trial[4:8] * trial[4:8] + trial[8:12] * trial[8:12])
    factor = radius / jnp.maximum(radius, length)
    factor_all = jnp.concatenate([factor, factor, factor], axis=0)
    active_all = jnp.concatenate([active, active, active], axis=0)
    cone = jnp.where(active_all == 1, tangent_mult - factor_all * trial, tangent_mult)
    gap = jnp.where(active == 1, wgap, normal_mult)
    return (gap, cone)


def live_slots(counts, slots, groups):
    cap = slots // groups
    index = jnp.arange(slots, dtype=jnp.int32)
    group_of = index // cap
    per_slot = jnp.sum(
        jnp.where(
            group_of[:, None] == jnp.arange(groups, dtype=jnp.int32)[None, :], counts[None, :], 0
        ),
        axis=1,
    )
    return index % cap < per_slot


def lookup(owner, offset, master_patch):
    count = owner.shape[0]
    peers = lax.axis_size("dev")
    sources = lax.axis_size("zone")
    width = sources * BUCKET
    block = count // sources
    peer_index = jnp.arange(peers, dtype=jnp.int32)
    hits = (owner.reshape(sources, block)[:, :, None] == peer_index[None, None, :]).astype(
        jnp.int32
    )
    before = jnp.cumsum(hits, axis=1) - hits
    rank = jnp.sum(before * hits, axis=2)
    position = (jnp.arange(sources, dtype=jnp.int32)[:, None] * BUCKET + rank).reshape(count)
    table = jnp.zeros((peers, width), jnp.int32).at[owner, position].set(offset)
    found = jnp.take(
        master_patch, lax.all_to_all(table, "dev", split_axis=0, concat_axis=0, tiled=True), axis=1
    )
    replies = lax.all_to_all(found, "dev", split_axis=1, concat_axis=1, tiled=True)
    flat = replies.reshape(12, peers * width)
    return jnp.take(flat, owner * width + position, axis=1)


def local(
    quad_weight,
    param_coords,
    slave_points,
    slave_normals,
    block_owner,
    block_patch,
    block_count,
    active_flags,
    normal_mult,
    tangent_mult,
    master_patch,
):
    groups = lax.axis_size("zone")
    slots = quad_weight.shape[0]
    mortar_d = slave_terms(quad_weight, param_coords)
    owner_ids = block_owner[:, 0]
    asked_owner, asked_patch = (
        lax.all_to_all(owner_ids, "zone", split_axis=0, concat_axis=0, tiled=True),
        lax.all_to_all(block_patch, "zone", split_axis=0, concat_axis=0, tiled=True),
    )
    found = lookup(asked_owner, asked_patch, master_patch)
    corners = lax.all_to_all(found, "zone", split_axis=1, concat_axis=1, tiled=True)
    back_m, back_gap, back_slip, back_lin = master_terms(
        quad_weight, param_coords, slave_points, slave_normals, corners
    )
    gap, cone = residuals(back_gap, back_slip, active_flags, normal_mult, tangent_mult)
    live = live_slots(block_count[0], slots, groups)[None]
    return (
        jnp.where(live, mortar_d, 0.0),
        jnp.where(live, back_m, 0.0),
        jnp.where(live, back_lin, 0.0),
        jnp.where(live, gap, 0.0),
        jnp.where(live, cone, 0.0),
    )


def solution(mesh):
    placed = (
        P(("zone", "dev"), None),
        P(("zone", "dev"), None, None),
        P(("zone", "dev"), None, None),
        P(("zone", "dev"), None, None),
        P(("zone", "dev"), None),
        P(("zone", "dev")),
        P(("zone", "dev"), None),
        P(None, ("zone", "dev")),
        P(None, ("zone", "dev")),
        P(None, ("zone", "dev")),
        P(None, ("zone", "dev")),
    )
    return jax.shard_map(
        local,
        mesh=mesh,
        in_specs=placed,
        out_specs=(
            P(None, ("zone", "dev")),
            P(None, ("zone", "dev")),
            P(None, ("zone", "dev")),
            P(None, ("zone", "dev")),
            P(None, ("zone", "dev")),
        ),
        check_vma=False,
    )
```

profile of v0, /device:TPU:0, one launch (start us, length us, event | category | flops | bytes accessed | tf_op | source)
XLA Modules:
  0.0 147.0 jit_solution(7890981640103569913)
XLA Ops:
  0.6 5.2 %all-to-all-start = ((s32[4,128,1]{1,2,0:T(1,128)}), s32[4,128,1]{1,2,0:T(1,128)S(1)}, u32[]{:S(2)}, u32[]{:S(2)}) async-start(s32[4,128,1]{1,2,0:T(1,128)} %bitcast.121), calls=%async_computation | async-start | bytes 4096 | tf_op jit(solution)/shard_map/all_to_all | solution.py:117
  5.8 3.4 %fusion.17 = (f32[512,1,128]{2,1,0:T(1,128)S(1)}, f32[512,1,128]{2,1,0:T(1,128)S(1)}, f32[512,1,128]{2,1,0:T(1,128)S(1)}, f32[512,1,128]{2,1,0:T(1,128)S(1)}) fusion(f32[512,4,128]{2,1,0:T(4,128)} %param.12), kind=kLoop, calls=%fused_computation.99 | loop fusion | bytes 2097152 | tf_op jit(solution)/shard_map/slice | solution.py:24
  9.2 1.2 slice_bitcast_fusion.1
  10.4 1.1 multiply_bitcast_fusion.3
  11.5 0.8 multiply_bitcast_fusion.7
  12.3 4.2 %all-to-all-start.1 = ((s32[4,128,1]{1,2,0:T(1,128)}), s32[4,128,1]{1,2,0:T(1,128)S(1)}, u32[]{:S(2)}, u32[]{:S(2)}) async-start(s32[4,128,1]{1,2,0:T(1,128)} %bitcast.18), calls=%async_computation.1 | async-start | bytes 4096 | tf_op jit(solution)/shard_map/all_to_all | solution.py:118
  17.2 3.8 %all-to-all-done.1 = s32[4,128,1]{1,2,0:T(1,128)S(1)} async-done(((s32[4,128,1]{1,2,0:T(1,128)}), s32[4,128,1]{1,2,0:T(1,128)S(1)}, u32[]{:S(2)}, u32[]{:S(2)}) %all-to-all-start.1) | async-done | bytes 2080 | tf_op jit(solution)/shard_map/all_to_all | solution.py:118
  21.6 76.9 %scatter_fusion = s32[8,64]{1,0:T(8,128)} fusion(s32[8,64]{1,0:T(8,128)} %broadcast_in_dim.120, s32[512]{0:T(512)S(1)} %bitcast.104, s32[512]{0:T(512)S(1)} %bitcast.118), kind=kCustom, calls=%fused_computation.2 | custom fusion | bytes 10240 | tf_op jit(solution)/shard_map/scatter | solution.py:90
  98.5 4.9 %all-to-all-start.2 = ((s32[8,1,64]{2,1,0:T(1,128)}), s32[8,1,64]{2,1,0:T(1,128)S(1)}, u32[]{:S(2)}, u32[]{:S(2)}) async-start(s32[8,1,64]{2,1,0:T(1,128)} %bitcast.21), calls=%async_computation.2 | async-start | bytes 8192 | tf_op jit(solution)/shard_map/all_to_all | solution.py:92
  103.5 3.6 %copy.70 = f32[12,8192]{0,1:T(8,128)} copy(f32[12,8192]{1,0:T(8,128)} %param.21) | data formatting | bytes 786432 | tf_op args[10]
  107.1 1.8 %all-to-all-done.2 = s32[8,1,64]{2,1,0:T(1,128)S(1)} async-done(((s32[8,1,64]{2,1,0:T(1,128)}), s32[8,1,64]{2,1,0:T(1,128)S(1)}, u32[]{:S(2)}, u32[]{:S(2)}) %all-to-all-start.2) | async-done | bytes 2080 | tf_op jit(solution)/shard_map/all_to_all | solution.py:92
  108.9 3.2 %gather_fusion = f32[512,12]{1,0:T(8,128)S(1)} fusion(f32[12,8192]{0,1:T(8,128)} %copy.70, s32[1024]{0:T(1024)S(1)} %pad_clamp_fusion.1), kind=kCustom, calls=%fused_computation | custom fusion | bytes 51200 | tf_op jit(solution)/shard_map/jit(_take)/gather | solution.py:91
  112.3 0.7 reshape.593
  113.0 3.3 %all-to-all-start.3 = ((f32[8,1,768]{2,1,0:T(1,128)}), f32[8,1,768]{2,1,0:T(1,128)S(1)}, u32[]{:S(2)}, u32[]{:S(2)}) async-start(f32[8,1,768]{2,1,0:T(1,128)} %reshape.593), calls=%async_computation.3 | async-start | bytes 49152 | tf_op jit(solution)/shard_map/all_to_all | solution.py:94
  116.4 5.7 %all-to-all-done.3 = f32[8,1,768]{2,1,0:T(1,128)S(1)} async-done(((f32[8,1,768]{2,1,0:T(1,128)}), f32[8,1,768]{2,1,0:T(1,128)S(1)}, u32[]{:S(2)}, u32[]{:S(2)}) %all-to-all-start.3) | async-done | bytes 24608 | tf_op jit(solution)/shard_map/all_to_all | solution.py:94
  122.6 0.7 reduce
  123.5 1.6 %gather_fusion.1 = f32[512,12]{1,0:T(8,128)} fusion(f32[12,512]{0,1:T(8,128)S(1)} %bitcast.105, s32[1024]{0:T(1024)S(1)} %pad_clamp_fusion), kind=kCustom, calls=%fused_computation.1 | custom fusion | bytes 51200 | tf_op jit(solution)/shard_map/jit(_take)/gather | solution.py:96
  125.2 1.1 copy.73
  126.9 3.3 %all-to-all-start.4 = ((f32[12,4,128]{2,0,1:T(8,128)}), f32[12,4,128]{2,0,1:T(8,128)S(1)}, u32[]{:S(2)}, u32[]{:S(2)}) async-start(f32[12,4,128]{2,0,1:T(8,128)} %broadcast_select_fusion), calls=%async_computation.4 | async-start | bytes 65536 | tf_op jit(solution)/shard_map/all_to_all | solution.py:121
  130.2 4.7 %all-to-all-done.4 = f32[12,4,128]{2,0,1:T(8,128)S(1)} async-done(((f32[12,4,128]{2,0,1:T(8,128)}), f32[12,4,128]{2,0,1:T(8,128)S(1)}, u32[]{:S(2)}, u32[]{:S(2)}) %all-to-all-start.4) | async-done | bytes 24608 | tf_op jit(solution)/shard_map/all_to_all | solution.py:121
  134.9 2.2 %multiply_reduce_fusion.6 = (f32[512,128]{1,0:T(8,128)S(1)}, f32[512,128]{1,0:T(8,128)S(1)}, f32[512,128]{1,0:T(8,128)S(1)}, f32[4,512,128]{2,1,0:T(8,128)S(1)}) fusion(f32[4,512]{1,0:T(4,128)S(1)} %get-tuple-element.42, f32[1,512,128]{2,1,0:T(8,128)} %get-tuple-element.39, f32[1,512,128]{2,1,0:T(8,128)} %get-tuple-element.40, ...), kind=kLoop, calls=%fused_computation.17 | loop fusion | flops 2162688 | bytes 2908160 | tf_op jit(solution)/shard_map/reduce_sum | solution.py:37
  137.4 1.3 multiply_reduce_fusion.4
  140.0 5.6 %fusion = (f32[4,4,512]{2,1,0:T(4,128)S(1)}, f32[4,4,512]{2,1,0:T(4,128)S(1)}, f32[4,4,512]{2,1,0:T(4,128)S(1)}, f32[4,4,512]{2,1,0:T(4,128)S(1)}, f32[4,4,512]{2,1,0:T(4,128)S(1)}) fusion(f32[512,128]{1,0:T(8,128)S(1)} %get-tuple-element.31, f32[4,512,128]{2,1,0:T(8,128)S(1)} %get-tuple-element.29, f32[4,512,128]{2,1,0:T(8,128)S(1)} %get-tuple-element.17, ...), kind=kLoop, calls=%fused_computation.7 | loop fusion | flops 10444800 | bytes 4096000 | tf_op jit(solution)/shard_map/reduce_sum | solution.py:46
  146.4 0.6 maximum_select_fusion
  (50 shorter events, 5.4 us)
Async XLA Ops:
  0.6 11.6 %all-to-all-start = ((s32[4,128,1]{1,2,0:T(1,128)}), s32[4,128,1]{1,2,0:T(1,128)S(1)}, u32[]{:S(2)}, u32[]{:S(2)}) async-start(s32[4,128,1]{1,2,0:T(1,128)} %bitcast.121), calls=%async_computation | async-start | bytes 4096 | tf_op jit(solution)/shard_map/all_to_all | solution.py:117
  10.4 93.0 %copy-start.7 = (s32[1,4]{1,0:T(1,128)S(1)}, s32[1,4]{1,0:T(1,128)}, u32[]{:S(2)}) copy-start(s32[1,4]{1,0:T(1,128)} %param.17) | copy-start | bytes 52
  12.3 8.8 %all-to-all-start.1 = ((s32[4,128,1]{1,2,0:T(1,128)}), s32[4,128,1]{1,2,0:T(1,128)S(1)}, u32[]{:S(2)}, u32[]{:S(2)}) async-start(s32[4,128,1]{1,2,0:T(1,128)} %bitcast.18), calls=%async_computation.1 | async-start | bytes 4096 | tf_op jit(solution)/shard_map/all_to_all | solution.py:118
  98.5 10.4 %all-to-all-start.2 = ((s32[8,1,64]{2,1,0:T(1,128)}), s32[8,1,64]{2,1,0:T(1,128)S(1)}, u32[]{:S(2)}, u32[]{:S(2)}) async-start(s32[8,1,64]{2,1,0:T(1,128)} %bitcast.21), calls=%async_computation.2 | async-start | bytes 8192 | tf_op jit(solution)/shard_map/all_to_all | solution.py:92
  103.5 33.6 %copy-start = (f32[512,3,128]{2,0,1:T(8,128)S(1)}, f32[512,3,128]{2,0,1:T(8,128)}, u32[]{:S(2)}) copy-start(f32[512,3,128]{2,0,1:T(8,128)} %param.14) | copy-start | bytes 2359300
  103.5 33.6 %copy-start.1 = (f32[512,3,128]{2,0,1:T(8,128)S(1)}, f32[512,3,128]{2,0,1:T(8,128)}, u32[]{:S(2)}) copy-start(f32[512,3,128]{2,0,1:T(8,128)} %param.13) | copy-start | bytes 2359300
  113.0 9.0 %all-to-all-start.3 = ((f32[8,1,768]{2,1,0:T(1,128)}), f32[8,1,768]{2,1,0:T(1,128)S(1)}, u32[]{:S(2)}, u32[]{:S(2)}) async-start(f32[8,1,768]{2,1,0:T(1,128)} %reshape.593), calls=%async_computation.3 | async-start | bytes 49152 | tf_op jit(solution)/shard_map/all_to_all | solution.py:94
  126.2 11.2 %copy-start.2 = (f32[1,512,128]{2,1,0:T(8,128)S(1)}, f32[1,512,128]{2,1,0:T(8,128)}, u32[]{:S(2)}) copy-start(f32[1,512,128]{2,1,0:T(8,128)} %get-tuple-element.36) | copy-start | bytes 786436
  126.9 8.0 %all-to-all-start.4 = ((f32[12,4,128]{2,0,1:T(8,128)}), f32[12,4,128]{2,0,1:T(8,128)S(1)}, u32[]{:S(2)}, u32[]{:S(2)}) async-start(f32[12,4,128]{2,0,1:T(8,128)} %broadcast_select_fusion), calls=%async_computation.4 | async-start | bytes 65536 | tf_op jit(solution)/shard_map/all_to_all | solution.py:121
  134.9 2.6 %copy-start.3 = (f32[512,128]{1,0:T(8,128)S(1)}, f32[512,128]{1,0:T(8,128)}, u32[]{:S(2)}) copy-start(f32[512,128]{1,0:T(8,128)} %param.11) | copy-start | bytes 786436
  137.1 1.6 %copy-start.4 = (f32[12,512]{1,0:T(8,128)S(1)}, f32[12,512]{1,0:T(8,128)}, u32[]{:S(2)}) copy-start(f32[12,512]{1,0:T(8,128)} %param.20) | copy-start | bytes 73732
  137.3 1.5 %copy-start.5 = (s32[4,512]{1,0:T(4,128)S(1)}, s32[4,512]{1,0:T(4,128)}, u32[]{:S(2)}) copy-start(s32[4,512]{1,0:T(4,128)} %param.18) | copy-start | bytes 24580
  137.3 1.5 %copy-start.6 = (f32[4,512]{1,0:T(4,128)S(1)}, f32[4,512]{1,0:T(4,128)}, u32[]{:S(2)}) copy-start(f32[4,512]{1,0:T(4,128)} %param.19) | copy-start | bytes 24580
where the time goes:
time: 149 us; the launch traced here: 147 us
  local copies, waits for them, and re-layouts  93.4 us (63%)
  starting transfers between devices  20.9 us (14%)
  other arithmetic  16 us (11%)
  waiting for transfers between devices  16 us (11%)
    scatter x1, local copies, waits for them, and re-layouts, lookup(): table = jnp.zeros((peers, width), jnp.int32).at[owner, position].set(offset)  76.9 us
    all_to_all x1, waiting for transfers between devices, lookup(): lax.all_to_all(found, 'dev', split_axis=1, concat_axis=1, tiled=True)  5.68 us
    reduce_sum x1, other arithmetic, master_terms(): jnp.sum(paired * normals[:, direction][None, None], axis=-1).reshape(16, -1)  5.61 us
    all_to_all x1, starting transfers between devices, local(): lax.all_to_all(owner_ids, 'zone', split_axis=0, concat_axis=0, tiled=True)  5.18 us
    all_to_all x1, starting transfers between devices, lookup(): lax.all_to_all(table, 'dev', split_axis=0, concat_axis=0, tiled=True)  4.88 us
    all_to_all x1, waiting for transfers between devices, local(): lax.all_to_all(found, 'zone', split_axis=1, concat_axis=1, tiled=True)  4.71 us
    unnamed x19, local copies, waits for them, and re-layouts  4.45 us
    all_to_all x1, starting transfers between devices, local(): lax.all_to_all(block_patch, 'zone', split_axis=0, concat_axis=0, tiled=True)  4.19 us
  transfers between devices with their start and end apart: 5, of which 4 were waited for; matrix products, arithmetic and copies ran while one was open for 7% of the time, Pallas kernels for 0%

commit v1 on v0

--- a/solution.py
+++ b/solution.py
@@ -91,7 +91,19 @@
     found = jnp.take(
         master_patch, lax.all_to_all(table, "dev", split_axis=0, concat_axis=0, tiled=True), axis=1
     )
-    replies = lax.all_to_all(found, "dev", split_axis=1, concat_axis=1, tiled=True)
+    ways, here = (lax.axis_size("dev"), lax.axis_index("dev"))
+    width_2 = found.shape[1] // ways
+    dims = list(found.shape)
+    dims[1] = width_2
+    height = dims[1]
+    dims[1] = height * ways
+    full = jnp.zeros(dims, found.dtype)
+    for mask in range(ways):
+        part = lax.dynamic_slice_in_dim(found, (here ^ mask) * width_2, width_2, axis=1)
+        if mask:
+            part = lax.ppermute(part, "dev", [(d, d ^ mask) for d in range(ways)])
+        full = lax.dynamic_update_slice_in_dim(full, part, (here ^ mask) * height, axis=1)
+    replies = full
     flat = replies.reshape(12, peers * width)
     return jnp.take(flat, owner * width + position, axis=1)
 

time: 149 us -> 157 us (1.054)
  starting transfers between devices: 20.9 us -> 25.8 us
  local copies, waits for them, and re-layouts: 93.4 us -> 97.9 us
  waiting for transfers between devices: 16 us -> 14 us
    ppermute x0 -> x7, starting transfers between devices: none -> 8.12 us  [lookup(): part = lax.ppermute(part, 'dev', [(d, d ^ mask) for d in range(ways)])]
    all_to_all x1 -> x0, waiting for transfers between devices: 5.68 us -> none  [lookup(): lax.all_to_all(found, 'dev', split_axis=1, concat_axis=1, tiled=True)]
    dynamic_update_slice x0 -> x8, local copies, waits for them, and re-layouts: none -> 4.84 us  [lookup(): lax.dynamic_update_slice_in_dim(full, part, (here ^ mask) * height, axis=1)]
    all_to_all x1, waiting for transfers between devices: 1.76 us -> 5.47 us  [lookup(): lax.all_to_all(table, 'dev', split_axis=0, concat_axis=0, tiled=True)]
    all_to_all x1 -> x0, starting transfers between devices: 3.34 us -> none  [lookup(): lax.all_to_all(found, 'dev', split_axis=1, concat_axis=1, tiled=True)]
    unnamed x19 -> x17, local copies, waits for them, and re-layouts: 4.45 us -> 2.65 us
    gather x2 -> x1, local copies, waits for them, and re-layouts: 3.36 us -> 3.83 us  [lookup(): jnp.take(master_patch, lax.all_to_all(table, 'dev', split_axis=0, concat_...]
  transfers between devices with their start and end apart: 5 -> 11, of which waited for: 4 -> 3; matrix products, arithmetic and copies ran while one was open for 7% -> 9% of each run, Pallas kernels for 0% -> 0%
where the time goes in v1:
time: 157 us; the launch traced here: 154 us
  local copies, waits for them, and re-layouts  97.9 us (62%)
  starting transfers between devices  25.8 us (16%)
  other arithmetic  15.6 us (10%)
  waiting for transfers between devices  14 us (9%)
    scatter x1, local copies, waits for them, and re-layouts, lookup(): table = jnp.zeros((peers, width), jnp.int32).at[owner, position].set(offset)  76.9 us
    ppermute x7, starting transfers between devices, lookup(): part = lax.ppermute(part, 'dev', [(d, d ^ mask) for d in range(ways)])  8.12 us
    reduce_sum x1, other arithmetic, master_terms(): jnp.sum(paired * normals[:, direction][None, None], axis=-1).reshape(16, -1)  5.61 us
    all_to_all x1, waiting for transfers between devices, lookup(): lax.all_to_all(table, 'dev', split_axis=0, concat_axis=0, tiled=True)  5.47 us
    all_to_all x1, starting transfers between devices, local(): lax.all_to_all(owner_ids, 'zone', split_axis=0, concat_axis=0, tiled=True)  5.31 us
    all_to_all x1, starting transfers between devices, lookup(): lax.all_to_all(table, 'dev', split_axis=0, concat_axis=0, tiled=True)  4.88 us
    dynamic_update_slice x8, local copies, waits for them, and re-layouts, lookup(): lax.dynamic_update_slice_in_dim(full, part, (here ^ mask) * height, axis=1)  4.84 us
    all_to_all x1, waiting for transfers between devices, local(): lax.all_to_all(found, 'zone', split_axis=1, concat_axis=1, tiled=True)  4.71 us
  transfers between devices with their start and end apart: 11, of which 3 were waited for; matrix products, arithmetic and copies ran while one was open for 9% of the time, Pallas kernels for 0%

profile of v1, /device:TPU:0, one launch (start us, length us, event | category | flops | bytes accessed | tf_op | source)
XLA Modules:
  0.0 154.2 jit_solution(824566327734965165)
XLA Ops:
  0.7 5.3 %all-to-all-start = ((s32[4,128,1]{1,2,0:T(1,128)}), s32[4,128,1]{1,2,0:T(1,128)S(1)}, u32[]{:S(2)}, u32[]{:S(2)}) async-start(s32[4,128,1]{1,2,0:T(1,128)} %bitcast.128), calls=%async_computation | async-start | bytes 4096 | tf_op jit(solution)/shard_map/all_to_all | solution.py:129
  6.0 3.4 %fusion.17 = (f32[512,1,128]{2,1,0:T(1,128)S(1)}, f32[512,1,128]{2,1,0:T(1,128)S(1)}, f32[512,1,128]{2,1,0:T(1,128)S(1)}, f32[512,1,128]{2,1,0:T(1,128)S(1)}) fusion(f32[512,4,128]{2,1,0:T(4,128)} %param.12), kind=kLoop, calls=%fused_computation.114 | loop fusion | bytes 2097152 | tf_op jit(solution)/shard_map/slice | solution.py:24
  9.4 1.2 slice_bitcast_fusion.1
  10.5 1.1 multiply_bitcast_fusion.3
  11.8 2.6 %copy.66 = f32[12,8192]{0,1:T(8,128)} copy(f32[12,8192]{1,0:T(8,128)S(1)} %copy-done.2) | data formatting | bytes 786432 | tf_op args[10]
  14.4 4.2 %all-to-all-start.1 = ((s32[4,128,1]{1,2,0:T(1,128)}), s32[4,128,1]{1,2,0:T(1,128)S(1)}, u32[]{:S(2)}, u32[]{:S(2)}) async-start(s32[4,128,1]{1,2,0:T(1,128)} %bitcast.18), calls=%async_computation.1 | async-start | bytes 4096 | tf_op jit(solution)/shard_map/all_to_all | solution.py:130
  19.4 3.8 %all-to-all-done.1 = s32[4,128,1]{1,2,0:T(1,128)S(1)} async-done(((s32[4,128,1]{1,2,0:T(1,128)}), s32[4,128,1]{1,2,0:T(1,128)S(1)}, u32[]{:S(2)}, u32[]{:S(2)}) %all-to-all-start.1) | async-done | bytes 2080 | tf_op jit(solution)/shard_map/all_to_all | solution.py:130
  23.8 76.9 %scatter_fusion = s32[8,64]{1,0:T(8,128)} fusion(s32[8,64]{1,0:T(8,128)} %broadcast_in_dim.124, s32[512]{0:T(512)S(1)} %bitcast.113, s32[512]{0:T(512)S(1)} %bitcast.125), kind=kCustom, calls=%fused_computation.2 | custom fusion | bytes 10240 | tf_op jit(solution)/shard_map/scatter | solution.py:90
  100.6 4.9 %all-to-all-start.2 = ((s32[8,1,64]{2,1,0:T(1,128)}), s32[8,1,64]{2,1,0:T(1,128)S(1)}, u32[]{:S(2)}, u32[]{:S(2)}) async-start(s32[8,1,64]{2,1,0:T(1,128)} %bitcast.21), calls=%async_computation.2 | async-start | bytes 8192 | tf_op jit(solution)/shard_map/all_to_all | solution.py:92
  105.5 5.5 %all-to-all-done.2 = s32[8,1,64]{2,1,0:T(1,128)S(1)} async-done(((s32[8,1,64]{2,1,0:T(1,128)}), s32[8,1,64]{2,1,0:T(1,128)S(1)}, u32[]{:S(2)}, u32[]{:S(2)}) %all-to-all-start.2) | async-done | bytes 2080 | tf_op jit(solution)/shard_map/all_to_all | solution.py:92
  111.1 3.8 %gather_fusion = f32[512,12]{1,0:T(8,128)} fusion(f32[12,8192]{0,1:T(8,128)} %copy.66, s32[1024]{0:T(1024)S(1)} %pad_clamp_fusion.1), kind=kCustom, calls=%fused_computation | custom fusion | bytes 51200 | tf_op jit(solution)/shard_map/jit(_take)/gather | solution.py:91
  114.9 1.1 broadcast_select_fusion
  116.8 1.2 collective-permute-start.2
  118.6 2.0 %collective-permute-start.4 = (f32[12,1,64]{0,2,1:T(8,128)S(1)}, f32[12,1,64]{0,2,1:T(8,128)S(1)}, u32[]{:S(2)}, u32[]{:S(2)}) collective-permute-start(f32[12,1,64]{0,2,1:T(8,128)S(1)} %get-tuple-element.43), channel_id=1, source_target_pairs={{0,5},{1,4},{2,7},{3,6},{4,1},{5,0},{6,3},{7,2},{8,13},{9,12},{10,... | collective-permute-start | bytes 9224 | tf_op jit(solution)/shard_map/ppermute | solution.py:104
  120.6 0.7 broadcast_in_dim.123
  123.1 3.0 %collective-permute-start.6 = (f32[12,1,64]{0,2,1:T(8,128)S(1)}, f32[12,1,64]{0,2,1:T(8,128)S(1)}, u32[]{:S(2)}, u32[]{:S(2)}) collective-permute-start(f32[12,1,64]{0,2,1:T(8,128)S(1)} %get-tuple-element.41), channel_id=1, source_target_pairs={{0,7},{1,6},{2,5},{3,4},{4,3},{5,2},{6,1},{7,0},{8,15},{9,14},{10,... | collective-permute-start | bytes 9224 | tf_op jit(solution)/shard_map/ppermute | solution.py:104
  129.8 2.6 %gather_fusion.1 = f32[512,12]{1,0:T(8,128)} fusion(f32[12,512]{0,1:T(8,128)} %bitcast.33, s32[1024]{0:T(1024)S(1)} %pad_clamp_fusion), kind=kCustom, calls=%fused_computation.1 | custom fusion | bytes 51200 | tf_op jit(solution)/shard_map/jit(_take)/gather | solution.py:108
  132.4 1.1 copy.67
  134.1 3.3 %all-to-all-start.3 = ((f32[12,4,128]{2,0,1:T(8,128)}), f32[12,4,128]{2,0,1:T(8,128)S(1)}, u32[]{:S(2)}, u32[]{:S(2)}) async-start(f32[12,4,128]{2,0,1:T(8,128)} %broadcast_select_fusion.1), calls=%async_computation.3 | async-start | bytes 65536 | tf_op jit(solution)/shard_map/all_to_all | solution.py:133
  137.3 4.7 %all-to-all-done.3 = f32[12,4,128]{2,0,1:T(8,128)S(1)} async-done(((f32[12,4,128]{2,0,1:T(8,128)}), f32[12,4,128]{2,0,1:T(8,128)S(1)}, u32[]{:S(2)}, u32[]{:S(2)}) %all-to-all-start.3) | async-done | bytes 24608 | tf_op jit(solution)/shard_map/all_to_all | solution.py:133
  142.1 2.2 %multiply_reduce_fusion.6 = (f32[512,128]{1,0:T(8,128)S(1)}, f32[512,128]{1,0:T(8,128)S(1)}, f32[512,128]{1,0:T(8,128)S(1)}, f32[4,512,128]{2,1,0:T(8,128)S(1)}) fusion(f32[4,512]{1,0:T(4,128)S(1)} %get-tuple-element.49, f32[1,512,128]{2,1,0:T(8,128)} %get-tuple-element.39, f32[1,512,128]{2,1,0:T(8,128)} %get-tuple-element.40, ...), kind=kLoop, calls=%fused_computation.17 | loop fusion | flops 2162688 | bytes 2908160 | tf_op jit(solution)/shard_map/reduce_sum | solution.py:37
  144.6 1.3 multiply_reduce_fusion.4
  147.2 5.6 %fusion = (f32[4,4,512]{2,1,0:T(4,128)S(1)}, f32[4,4,512]{2,1,0:T(4,128)S(1)}, f32[4,4,512]{2,1,0:T(4,128)S(1)}, f32[4,4,512]{2,1,0:T(4,128)S(1)}, f32[4,4,512]{2,1,0:T(4,128)S(1)}) fusion(f32[512,128]{1,0:T(8,128)S(1)} %get-tuple-element.31, f32[4,512,128]{2,1,0:T(8,128)S(1)} %get-tuple-element.29, f32[4,512,128]{2,1,0:T(8,128)S(1)} %get-tuple-element.17, ...), kind=kLoop, calls=%fused_computation.7 | loop fusion | flops 10444800 | bytes 4096000 | tf_op jit(solution)/shard_map/reduce_sum | solution.py:46
  153.5 0.6 maximum_select_fusion
  (66 shorter events, 11.3 us)
Async XLA Ops:
  0.6 11.1 %copy-start.7 = (s32[1,4]{1,0:T(1,128)S(1)}, s32[1,4]{1,0:T(1,128)}, u32[]{:S(2)}) copy-start(s32[1,4]{1,0:T(1,128)} %param.17) | copy-start | bytes 52
  0.6 11.1 %copy-start.2 = (f32[12,8192]{1,0:T(8,128)S(1)}, f32[12,8192]{1,0:T(8,128)}, u32[]{:S(2)}) copy-start(f32[12,8192]{1,0:T(8,128)} %param.21) | copy-start | bytes 1179652
  0.7 13.8 %all-to-all-start = ((s32[4,128,1]{1,2,0:T(1,128)}), s32[4,128,1]{1,2,0:T(1,128)S(1)}, u32[]{:S(2)}, u32[]{:S(2)}) async-start(s32[4,128,1]{1,2,0:T(1,128)} %bitcast.128), calls=%async_computation | async-start | bytes 4096 | tf_op jit(solution)/shard_map/all_to_all | solution.py:129
  14.4 8.8 %all-to-all-start.1 = ((s32[4,128,1]{1,2,0:T(1,128)}), s32[4,128,1]{1,2,0:T(1,128)S(1)}, u32[]{:S(2)}, u32[]{:S(2)}) async-start(s32[4,128,1]{1,2,0:T(1,128)} %bitcast.18), calls=%async_computation.1 | async-start | bytes 4096 | tf_op jit(solution)/shard_map/all_to_all | solution.py:130
  23.8 120.5 %copy-start = (f32[512,3,128]{2,0,1:T(8,128)S(1)}, f32[512,3,128]{2,0,1:T(8,128)}, u32[]{:S(2)}) copy-start(f32[512,3,128]{2,0,1:T(8,128)} %param.14) | copy-start | bytes 2359300
  23.8 120.5 %copy-start.1 = (f32[512,3,128]{2,0,1:T(8,128)S(1)}, f32[512,3,128]{2,0,1:T(8,128)}, u32[]{:S(2)}) copy-start(f32[512,3,128]{2,0,1:T(8,128)} %param.13) | copy-start | bytes 2359300
  100.6 10.4 %all-to-all-start.2 = ((s32[8,1,64]{2,1,0:T(1,128)}), s32[8,1,64]{2,1,0:T(1,128)S(1)}, u32[]{:S(2)}, u32[]{:S(2)}) async-start(s32[8,1,64]{2,1,0:T(1,128)} %bitcast.21), calls=%async_computation.2 | async-start | bytes 8192 | tf_op jit(solution)/shard_map/all_to_all | solution.py:92
  116.1 5.9 %collective-permute-start = (f32[12,1,64]{0,2,1:T(8,128)S(1)}, f32[12,1,64]{0,2,1:T(8,128)S(1)}, u32[]{:S(2)}, u32[]{:S(2)}) collective-permute-start(f32[12,1,64]{0,2,1:T(8,128)S(1)} %get-tuple-element.47), channel_id=1, source_target_pairs={{0,1},{1,0},{2,3},{3,2},{4,5},{5,4},{6,7},{7,6},{8,9},{9,8},{10,11... | collective-permute-start | bytes 9224 | tf_op jit(solution)/shard_map/ppermute | solution.py:104
  116.1 6.9 %collective-permute-start.1 = (f32[12,1,64]{0,2,1:T(8,128)S(1)}, f32[12,1,64]{0,2,1:T(8,128)S(1)}, u32[]{:S(2)}, u32[]{:S(2)}) collective-permute-start(f32[12,1,64]{0,2,1:T(8,128)S(1)} %get-tuple-element.46), channel_id=1, source_target_pairs={{0,2},{1,3},{2,0},{3,1},{4,6},{5,7},{6,4},{7,5},{8,10},{9,11},{10,... | collective-permute-start | bytes 9224 | tf_op jit(solution)/shard_map/ppermute | solution.py:104
  116.8 9.9 %collective-permute-start.2 = (f32[12,1,64]{0,2,1:T(8,128)S(1)}, f32[12,1,64]{0,2,1:T(8,128)S(1)}, u32[]{:S(2)}, u32[]{:S(2)}) collective-permute-start(f32[12,1,64]{0,2,1:T(8,128)S(1)} %get-tuple-element.45), channel_id=1, source_target_pairs={{0,3},{1,2},{2,1},{3,0},{4,7},{5,6},{6,5},{7,4},{8,11},{9,10},{10,... | collective-permute-start | bytes 9224 | tf_op jit(solution)/shard_map/ppermute | solution.py:104
  118.0 9.3 %collective-permute-start.3 = (f32[12,1,64]{0,2,1:T(8,128)S(1)}, f32[12,1,64]{0,2,1:T(8,128)S(1)}, u32[]{:S(2)}, u32[]{:S(2)}) collective-permute-start(f32[12,1,64]{0,2,1:T(8,128)S(1)} %get-tuple-element.44), channel_id=1, source_target_pairs={{0,4},{1,5},{2,6},{3,7},{4,0},{5,1},{6,2},{7,3},{8,12},{9,13},{10,... | collective-permute-start | bytes 9224 | tf_op jit(solution)/shard_map/ppermute | solution.py:104
  118.6 9.4 %collective-permute-start.4 = (f32[12,1,64]{0,2,1:T(8,128)S(1)}, f32[12,1,64]{0,2,1:T(8,128)S(1)}, u32[]{:S(2)}, u32[]{:S(2)}) collective-permute-start(f32[12,1,64]{0,2,1:T(8,128)S(1)} %get-tuple-element.43), channel_id=1, source_target_pairs={{0,5},{1,4},{2,7},{3,6},{4,1},{5,0},{6,3},{7,2},{8,13},{9,12},{10,... | collective-permute-start | bytes 9224 | tf_op jit(solution)/shard_map/ppermute | solution.py:104
  121.9 6.6 %collective-permute-start.5 = (f32[12,1,64]{0,2,1:T(8,128)S(1)}, f32[12,1,64]{0,2,1:T(8,128)S(1)}, u32[]{:S(2)}, u32[]{:S(2)}) collective-permute-start(f32[12,1,64]{0,2,1:T(8,128)S(1)} %get-tuple-element.42), channel_id=1, source_target_pairs={{0,6},{1,7},{2,4},{3,5},{4,2},{5,3},{6,0},{7,1},{8,14},{9,15},{10,... | collective-permute-start | bytes 9224 | tf_op jit(solution)/shard_map/ppermute | solution.py:104
  123.1 6.1 %collective-permute-start.6 = (f32[12,1,64]{0,2,1:T(8,128)S(1)}, f32[12,1,64]{0,2,1:T(8,128)S(1)}, u32[]{:S(2)}, u32[]{:S(2)}) collective-permute-start(f32[12,1,64]{0,2,1:T(8,128)S(1)} %get-tuple-element.41), channel_id=1, source_target_pairs={{0,7},{1,6},{2,5},{3,4},{4,3},{5,2},{6,1},{7,0},{8,15},{9,14},{10,... | collective-permute-start | bytes 9224 | tf_op jit(solution)/shard_map/ppermute | solution.py:104
  134.1 8.0 %all-to-all-start.3 = ((f32[12,4,128]{2,0,1:T(8,128)}), f32[12,4,128]{2,0,1:T(8,128)S(1)}, u32[]{:S(2)}, u32[]{:S(2)}) async-start(f32[12,4,128]{2,0,1:T(8,128)} %broadcast_select_fusion.1), calls=%async_computation.3 | async-start | bytes 65536 | tf_op jit(solution)/shard_map/all_to_all | solution.py:133
  142.1 2.6 %copy-start.3 = (f32[512,128]{1,0:T(8,128)S(1)}, f32[512,128]{1,0:T(8,128)}, u32[]{:S(2)}) copy-start(f32[512,128]{1,0:T(8,128)} %param.11) | copy-start | bytes 786436
  144.3 1.6 %copy-start.4 = (f32[12,512]{1,0:T(8,128)S(1)}, f32[12,512]{1,0:T(8,128)}, u32[]{:S(2)}) copy-start(f32[12,512]{1,0:T(8,128)} %param.20) | copy-start | bytes 73732
  144.5 1.5 copy-start.5
  144.5 1.5 copy-start.6
